TPU v7x, 32 devices: a whole 2x2x4 slice. The times are simulated.
32 devices in a mesh: tm: 16 (over z, y, core), series: 2 (over x).
Axes of the slice: x: 2, y: 2, z: 4, core: 2. Of those that a mesh axis runs over, the one named last changes fastest.
Arguments:
- panel: bfloat16 [4096, 16384], P('series', 'tm'), may hold values from -6 to 6
- series_factors: bfloat16 [4096, 128], P('series'), may hold values from -1.796875 to 1.796875
- time_factors: bfloat16 [16384, 128], P('tm'), may hold values from -1.796875 to 1.796875
- ar_weights: float32 [16, 128], replicated, may hold values from -1 to 1
- tile_mask: int32 [32, 128], P('series', 'tm'), may hold values 0 or 1
- lags: int32 [16], replicated, may hold values from 1 to 128, as said below
Outputs:
- series_grad: float32 [4096, 128], P(('series', 'tm'))
- time_grad: float32 [16384, 128], P(('tm', 'series'))
- ar_grad: float32 [16, 128], replicated
Inputs may be any that keep to these rules, and one draw needn't show every extreme that they name: `lags`: strictly increasing, and the last equals 128.
All inputs are finite; a program needn't handle non-finite values. No bound on the sum of `tile_mask` on one device may be relied on, other than what follows from the above.
Results may differ from a plain program's by a relative error of at most 0.00045.
Values may be sent and summed in bfloat16 or wider, within the bound.
A program may use at most 64 MiB of HBM per device.

v0:
```python
import math
import jax
import jax.numpy as jnp
from jax import lax
from jax.sharding import PartitionSpec as P

NLAG = 16
LAGMAX = 128
TILE = 128
ar_strength = 1.0


def from_behind(value, axis, steps):
    count = lax.axis_size(axis)
    initial, last = (max(0, -steps), min(count, count - steps))
    return lax.ppermute(value, axis, [(source, source + steps) for source in range(initial, last)])


def lag_error(extended, weights, lags, count):
    total = extended[LAGMAX : LAGMAX + count]
    for lag_pos in range(NLAG):
        shifted = lax.dynamic_slice_in_dim(extended, LAGMAX - lags[lag_pos], count, 0)
        total = total - weights[lag_pos] * shifted
    return total


def per_device(panel, series_factors, time_factors, ar_weights, tile_mask, lags):
    time_rows = time_factors.shape[0]
    series_rows = series_factors.shape[0]
    time_devices = lax.axis_size("tm")
    series_devices = lax.axis_size("series")
    scale_time = 1.0 / math.sqrt(time_rows * time_devices)
    scale_series = 1.0 / math.sqrt(series_rows * series_devices)
    tm_index = lax.axis_index("tm")
    earlier = from_behind(time_factors[time_rows - LAGMAX :], "tm", 1)
    keep = jnp.repeat(jnp.repeat(tile_mask, TILE, 0), TILE, 1) > 0
    predicted = jnp.dot(series_factors, time_factors.T, preferred_element_type=jnp.float32)
    residual = jnp.where(keep, predicted - panel.astype(jnp.float32), jnp.float32(0.0)).astype(
        jnp.bfloat16
    )
    series_part = jnp.dot(residual, time_factors, preferred_element_type=jnp.float32) * scale_time
    time_part = (
        lax.dot_general(
            residual, series_factors, (((0,), (0,)), ((), ())), preferred_element_type=jnp.float32
        )
        * scale_series
    )
    factors32 = time_factors.astype(jnp.float32)
    extended = jnp.concatenate([earlier.astype(jnp.float32), factors32], axis=0)
    moments = tm_index * time_rows + jnp.arange(time_rows, dtype=jnp.int32)
    error = jnp.where(
        (moments >= LAGMAX)[:, None],
        lag_error(extended, ar_weights, lags, time_rows),
        jnp.float32(0.0),
    )
    upcoming = from_behind(error[:LAGMAX].astype(jnp.bfloat16), "tm", -1).astype(jnp.float32)
    error_ext = jnp.concatenate([error, upcoming], axis=0)
    adjoint = error
    ar_rows = []
    for lag_pos in range(NLAG):
        ahead = lax.dynamic_slice_in_dim(error_ext, lags[lag_pos], time_rows, 0)
        adjoint = adjoint - ar_weights[lag_pos] * ahead
        behind = lax.dynamic_slice_in_dim(extended, LAGMAX - lags[lag_pos], time_rows, 0)
        ar_rows.append(-scale_time * jnp.sum(error * behind, axis=0))
    ar_part = jnp.stack(ar_rows)
    series_grad = lax.psum_scatter(series_part, "tm", scatter_dimension=0, tiled=True)
    ar_grad = lax.psum(ar_part, "tm")
    time_share = lax.psum_scatter(time_part, "series", scatter_dimension=0, tiled=True)
    own_time = time_rows // series_devices
    adjoint_rows = lax.dynamic_slice_in_dim(
        adjoint, lax.axis_index("series") * own_time, own_time, 0
    )
    time_grad = time_share + ar_strength * adjoint_rows
    return (series_grad, time_grad, ar_grad)


def solution(mesh):
    in_specs = (P("series", "tm"), P("series", None), P("tm", None), P(), P("series", "tm"), P())
    out_specs = (P(("series", "tm"), None), P(("tm", "series"), None), P())
    return jax.shard_map(
        per_device, mesh=mesh, in_specs=in_specs, out_specs=out_specs, check_vma=False
    )
```

profile of v0, /device:TPU:0, one launch (start us, length us, event | category | flops | bytes accessed | tf_op | source)
XLA Modules:
  0.0 137.6 jit_solution(11205370588736498086)
XLA Ops:
  7.2 0.0 reduce-scatter.5.cloned.1.call-start
  7.2 0.7 broadcast_compare_fusion
  8.0 0.1 copy.9
  8.1 0.1 broadcast_in_dim.23
  8.1 6.4 %broadcast_in_dim.24 = pred[2048,8,128]{2,1,0:T(8,128)(4,1)S(1)} broadcast(pred[2048,8]{1,0:T(8,128)(4,1)S(1)} %bitcast.91), dimensions={0,1} | broadcast | bytes 2113536 | tf_op jit(solution)/shard_map/broadcast_in_dim | solution.py:36
  14.5 4.1 %select_convert_fusion = bf16[2048,1024]{1,0:T(8,128)(2,1)S(1)} fusion(bf16[2048,1024]{1,0:T(8,128)(2,1)} %param.6, pred[256,8,8,128]{3,2,1,0:T(8,128)(4,1)S(1)} %bitcast.90, bf16[2048,128]{1,0:T(8,128)(2,1)S(1)} %copy-done, bf16[1024,128]{1,0:T(8,128)(2,1)} %param.8), kind=kOutput, calls=%fused_computation | convolution fusion | flops 545259520 | bytes 11272192 | tf_op jit(solution)/shard_map/dot_general | solution.py:37
  18.6 1.9 %copy-done.1 = bf16[2048,1024]{1,0:T(8,128)(2,1)} copy-done((bf16[2048,1024]{1,0:T(8,128)(2,1)}, bf16[2048,1024]{1,0:T(8,128)(2,1)S(1)}, u32[]{:S(2)}) %copy-start.1) | copy-done | bytes 4194328
  20.5 2.1 %convolution_multiply_fusion.1 = f32[1024,128]{1,0:T(8,128)} fusion(bf16[2048,1024]{1,0:T(8,128)(2,1)S(1)} %select_convert_fusion, bf16[2048,128]{1,0:T(8,128)(2,1)S(1)} %copy-done), kind=kOutput, calls=%fused_computation.34 | convolution fusion | flops 537001984 | bytes 5242880 | tf_op jit(solution)/shard_map/dot_general | solution.py:43
  22.6 0.0 reduce-scatter.5.cloned.1.call-update
  22.6 0.0 reduce-scatter.3.cloned.1.call-start
  22.7 2.4 %collective-permute-start = (bf16[128,128]{1,0:T(8,128)(2,1)S(1)}, bf16[128,128]{1,0:T(8,128)(2,1)S(1)}, u32[]{:S(2)}, u32[]{:S(2)}) collective-permute-start(bf16[128,128]{1,0:T(8,128)(2,1)S(1)} %slice.70), channel_id=1, source_target_pairs={{0,2},{2,4},{4,6},{6,8},{8,10},{10,12},{12,14},{14,16},{16,18},{18... | collective-permute-start | bytes 98312 | tf_op jit(solution)/shard_map/ppermute | solution.py:16
  25.1 4.4 %convolution_multiply_fusion = f32[2048,128]{1,0:T(8,128)} fusion(bf16[2048,1024]{1,0:T(8,128)(2,1)} %copy-done.1, bf16[1024,128]{1,0:T(8,128)(2,1)S(1)} %copy-done.2), kind=kOutput, calls=%fused_computation.33 | convolution fusion | flops 537133056 | bytes 5505024 | tf_op jit(solution)/shard_map/dot_general | solution.py:41
  29.5 0.0 reduce-scatter.3.cloned.1.call-update
  29.6 0.7 fusion.63
  80.7 4.1 %multiply_reduce_fusion = (f32[128]{0:T(128)S(1)}, f32[128]{0:T(128)S(1)}, f32[128]{0:T(128)S(1)}, f32[128]{0:T(128)S(1)}, f32[128]{0:T(128)S(1)}, /*index=5*/f32[128]{0:T(128)S(1)}, f32[1024,128]{1,0:T(8,128)S(1)}) fusion(s32[]{:T(128)S(6)} %select_n.139, f32[1024,128]{1,0:T(8,128)S(1)} %convert_element_type.18, f32[128,128]{1,0:T(8,128)S(1)} %convert_element_type.19, ...), kind=kLoop, calls=%fused_computation.116 | loop fusion | flops 8912128 | bytes 1388608 | tf_op jit(solution)/shard_map/reduce_sum | solution.py:64
  84.8 0.5 multiply_reduce_fusion.12
  85.3 0.7 multiply_reduce_fusion.6
  86.0 1.3 collective-permute-start.1
  87.4 0.1 stack.2
  87.5 37.2 %psum.7 = f32[16,128]{1,0:T(8,128)} all-reduce(f32[16,128]{1,0:T(8,128)S(1)} %stack.2), channel_id=1, replica_groups=mesh['tm'=16,'series'=2] {'tm'}, use_global_device_ids=true, to_apply=%region_18.19 | all-reduce | flops 2048 | bytes 16384 | tf_op jit(solution)/shard_map/psum | solution.py:67
  124.6 0.5 fusion.31
  125.2 3.3 %fusion.11 = f32[1024,128]{1,0:T(8,128)S(1)} fusion(f32[1024,128]{1,0:T(8,128)S(1)} %get-tuple-element.19, s32[]{:T(128)S(6)} %select_n.141, s32[]{:T(128)S(6)} %select_n.142, s32[]{:T(128)S(6)} %select_n.143, s32[]{:T(128)S(6)} %select_n.144, s32[]{:T(128)S(6)} %select_n.145, s32[]{:T(128)S(6)} %select_n.146, s32[]{:T(128)S(6)} %select_n.147, ...), kind=kLoop, calls=%fused_computation.78 | loop fusion | flops 3932160 | bytes 1119272 | tf_op jit(solution)/shard_map/sub | solution.py:62
  128.4 0.0 reduce-scatter.5.cloned.1.call-done
  128.5 2.2 %fusion.52 = f32[512,128]{1,0:T(8,128)} fusion(f32[512,128]{1,0:T(8,128)} %reduce-scatter.5.cloned.1.call-done, s32[]{:T(128)S(6)} %add.192, f32[1024,128]{1,0:T(8,128)S(1)} %get-tuple-element.19, s32[]{:T(128)S(6)} %add.186, s32[]{:T(128)S(6)} %add.188, s32[]{:T(128)S(6)} %add.190, f32[128,128]{1,0:T(8,128)S(1)} %convert_element_type.20, ...), kind=kLoop, calls=%fused_computation.136 | loop fusion | flops 1048576 | bytes 1903124 | tf_op jit(solution)/shard_map/add | solution.py:73
  (27 shorter events, 0.1 us)
Async XLA Ops:
  7.2 7.3 %copy-start = (bf16[2048,128]{1,0:T(8,128)(2,1)S(1)}, bf16[2048,128]{1,0:T(8,128)(2,1)}, u32[]{:S(2)}) copy-start(bf16[2048,128]{1,0:T(8,128)(2,1)} %param.7) | copy-start | bytes 1572868
  7.2 121.3 %reduce-scatter.5.cloned.1.call-start = ((), (), s32[]{:S(2)}) async-start(), calls=%async_computation.3 | async-start | bytes 786432 | tf_op jit(solution)/shard_map/reduce_scatter | solution.py:68
  18.6 1.9 %copy-start.1 = (bf16[2048,1024]{1,0:T(8,128)(2,1)}, bf16[2048,1024]{1,0:T(8,128)(2,1)S(1)}, u32[]{:S(2)}) copy-start(bf16[2048,1024]{1,0:T(8,128)(2,1)S(1)} %select_convert_fusion) | copy-start | bytes 12582916
  20.5 2.2 %copy-start.2 = (bf16[1024,128]{1,0:T(8,128)(2,1)S(1)}, bf16[1024,128]{1,0:T(8,128)(2,1)}, u32[]{:S(2)}) copy-start(bf16[1024,128]{1,0:T(8,128)(2,1)} %param.8) | copy-start | bytes 786436
  22.6 7.0 %copy-start.3 = (s32[16]{0:T(128)S(1)}, s32[16]{0:T(128)}, u32[]{:S(2)}) copy-start(s32[16]{0:T(128)} %param.11) | copy-start | bytes 196
  22.6 7.7 %copy-start.4 = (f32[16,128]{1,0:T(8,128)S(1)}, f32[16,128]{1,0:T(8,128)}, u32[]{:S(2)}) copy-start(f32[16,128]{1,0:T(8,128)} %param.9) | copy-start | bytes 24580
  22.6 108.1 %reduce-scatter.3.cloned.1.call-start = ((), (), s32[]{:S(2)}) async-start(), calls=%async_computation.2 | async-start | bytes 1114112 | tf_op jit(solution)/shard_map/reduce_scatter | solution.py:66
  22.7 58.0 %collective-permute-start = (bf16[128,128]{1,0:T(8,128)(2,1)S(1)}, bf16[128,128]{1,0:T(8,128)(2,1)S(1)}, u32[]{:S(2)}, u32[]{:S(2)}) collective-permute-start(bf16[128,128]{1,0:T(8,128)(2,1)S(1)} %slice.70), channel_id=1, source_target_pairs={{0,2},{2,4},{4,6},{6,8},{8,10},{10,12},{12,14},{14,16},{16,18},{18... | collective-permute-start | bytes 98312 | tf_op jit(solution)/shard_map/ppermute | solution.py:16
  86.0 38.6 %collective-permute-start.1 = (bf16[128,128]{1,0:T(8,128)(2,1)S(1)}, bf16[128,128]{1,0:T(8,128)(2,1)S(1)}, u32[]{:S(2)}, u32[]{:S(2)}) collective-permute-start(bf16[128,128]{1,0:T(8,128)(2,1)S(1)} %slice.203), channel_id=1, source_target_pairs={{2,0},{4,2},{6,4},{8,6},{10,8},{12,10},{14,12},{16,14},{18,16},{20... | collective-permute-start | bytes 98312 | tf_op jit(solution)/shard_map/ppermute | solution.py:16
Sparse Core Ops, SparseCore 0:
  22.8 17.3 reduce-scatter.4
  44.3 57.6 reduce-scatter.2
where the time goes:
time: 139 us; the launch traced here: 138 us
  between operations  64.6 us (46%)
  blocking collectives  37.2 us (27%)
  other arithmetic  12.2 us (9%)
  matrix products  10.6 us (8%)
  local copies, waits for them, and re-layouts  9.25 us (7%)
  starting transfers between devices  3.77 us (3%)
    psum x1, blocking collectives, per_device(): ar_grad = lax.psum(ar_part, 'tm')  37.2 us
    broadcast_in_dim x2, local copies, waits for them, and re-layouts, per_device(): keep = jnp.repeat(jnp.repeat(tile_mask, TILE, 0), TILE, 1) > 0  6.44 us
    reduce_sum x3, other arithmetic, per_device(): ar_rows.append(-scale_time * jnp.sum(error * behind, axis=0))  5.29 us
    dot_general x1, matrix products, per_device(): jnp.dot(residual, time_factors, preferred_element_type=jnp.float32)  4.42 us
    dot_general x1, matrix products, per_device(): jnp.dot(series_factors, time_factors.T, preferred_element_type=jnp.float32)  4.07 us
    ppermute x2, starting transfers between devices, from_behind(): lax.ppermute(value, axis, [(source, source + steps) for source in range(i...  3.69 us
    sub x1, other arithmetic, per_device(): adjoint = adjoint - ar_weights[lag_pos] * ahead  3.26 us
  transfers between devices with their start and end apart: 4, of which 0 were waited for; matrix products, arithmetic and copies ran while one was open for 12% of the time, Pallas kernels for 0%

commit v1 on v0

--- a/solution.py
+++ b/solution.py
@@ -64,7 +64,8 @@
         ar_rows.append(-scale_time * jnp.sum(error * behind, axis=0))
     ar_part = jnp.stack(ar_rows)
     series_grad = lax.psum_scatter(series_part, "tm", scatter_dimension=0, tiled=True)
-    ar_grad = lax.psum(ar_part, "tm")
+    terms = lax.all_gather(ar_part, "tm")
+    ar_grad = jnp.sum(terms, axis=0)
     time_share = lax.psum_scatter(time_part, "series", scatter_dimension=0, tiled=True)
     own_time = time_rows // series_devices
     adjoint_rows = lax.dynamic_slice_in_dim(

time: 139 us -> 128 us (0.921)
  blocking collectives: 37.2 us -> 25.5 us
    psum x1 -> x0, blocking collectives: 37.2 us -> none  [per_device(): ar_grad = lax.psum(ar_part, 'tm')]
    all_gather x0 -> x1, blocking collectives: none -> 25.5 us  [per_device(): terms = lax.all_gather(ar_part, 'tm')]
  transfers between devices with their start and end apart: 4 -> 4, of which waited for: 0 -> 0; matrix products, arithmetic and copies ran while one was open for 12% -> 14% of each run, Pallas kernels for 0% -> 0%
where the time goes in v1:
time: 128 us; the launch traced here: 127 us
  between operations  64.6 us (50%)
  blocking collectives  25.5 us (20%)
  other arithmetic  12.8 us (10%)
  matrix products  10.6 us (8%)
  local copies, waits for them, and re-layouts  9.25 us (7%)
  starting transfers between devices  3.77 us (3%)
    all_gather x1, blocking collectives, per_device(): terms = lax.all_gather(ar_part, 'tm')  25.5 us
    broadcast_in_dim x2, local copies, waits for them, and re-layouts, per_device(): keep = jnp.repeat(jnp.repeat(tile_mask, TILE, 0), TILE, 1) > 0  6.44 us
    reduce_sum x3, other arithmetic, per_device(): ar_rows.append(-scale_time * jnp.sum(error * behind, axis=0))  5.29 us
    dot_general x1, matrix products, per_device(): jnp.dot(residual, time_factors, preferred_element_type=jnp.float32)  4.42 us
    dot_general x1, matrix products, per_device(): jnp.dot(series_factors, time_factors.T, preferred_element_type=jnp.float32)  4.07 us
    ppermute x2, starting transfers between devices, from_behind(): lax.ppermute(value, axis, [(source, source + steps) for source in range(i...  3.69 us
    sub x1, other arithmetic, per_device(): adjoint = adjoint - ar_weights[lag_pos] * ahead  3.26 us
  transfers between devices with their start and end apart: 4, of which 0 were waited for; matrix products, arithmetic and copies ran while one was open for 14% of the time, Pallas kernels for 0%

profile of v1, /device:TPU:0, one launch (start us, length us, event | category | flops | bytes accessed | tf_op | source)
XLA Modules:
  0.0 126.5 jit_solution(11393759370098559169)
XLA Ops:
  7.2 0.0 reduce-scatter.5.cloned.1.call-start
  7.2 0.7 broadcast_compare_fusion
  8.0 0.1 copy.9
  8.1 0.1 broadcast_in_dim.23
  8.1 6.4 %broadcast_in_dim.24 = pred[2048,8,128]{2,1,0:T(8,128)(4,1)S(1)} broadcast(pred[2048,8]{1,0:T(8,128)(4,1)S(1)} %bitcast.92), dimensions={0,1} | broadcast | bytes 2113536 | tf_op jit(solution)/shard_map/broadcast_in_dim | solution.py:36
  14.5 4.1 %select_convert_fusion = bf16[2048,1024]{1,0:T(8,128)(2,1)S(1)} fusion(bf16[2048,1024]{1,0:T(8,128)(2,1)} %param.6, pred[256,8,8,128]{3,2,1,0:T(8,128)(4,1)S(1)} %bitcast.91, bf16[2048,128]{1,0:T(8,128)(2,1)S(1)} %copy-done, bf16[1024,128]{1,0:T(8,128)(2,1)} %param.8), kind=kOutput, calls=%fused_computation | convolution fusion | flops 545259520 | bytes 11272192 | tf_op jit(solution)/shard_map/dot_general | solution.py:37
  18.6 1.9 %copy-done.1 = bf16[2048,1024]{1,0:T(8,128)(2,1)} copy-done((bf16[2048,1024]{1,0:T(8,128)(2,1)}, bf16[2048,1024]{1,0:T(8,128)(2,1)S(1)}, u32[]{:S(2)}) %copy-start.1) | copy-done | bytes 4194328
  20.5 2.1 %convolution_multiply_fusion.1 = f32[1024,128]{1,0:T(8,128)} fusion(bf16[2048,1024]{1,0:T(8,128)(2,1)S(1)} %select_convert_fusion, bf16[2048,128]{1,0:T(8,128)(2,1)S(1)} %copy-done), kind=kOutput, calls=%fused_computation.34 | convolution fusion | flops 537001984 | bytes 5242880 | tf_op jit(solution)/shard_map/dot_general | solution.py:43
  22.6 0.0 reduce-scatter.3.cloned.1.call-start
  22.7 2.4 %collective-permute-start = (bf16[128,128]{1,0:T(8,128)(2,1)S(1)}, bf16[128,128]{1,0:T(8,128)(2,1)S(1)}, u32[]{:S(2)}, u32[]{:S(2)}) collective-permute-start(bf16[128,128]{1,0:T(8,128)(2,1)S(1)} %slice.70), channel_id=1, source_target_pairs={{0,2},{2,4},{4,6},{6,8},{8,10},{10,12},{12,14},{14,16},{16,18},{18... | collective-permute-start | bytes 98312 | tf_op jit(solution)/shard_map/ppermute | solution.py:16
  25.1 4.4 %convolution_multiply_fusion = f32[2048,128]{1,0:T(8,128)} fusion(bf16[2048,1024]{1,0:T(8,128)(2,1)} %copy-done.1, bf16[1024,128]{1,0:T(8,128)(2,1)S(1)} %copy-done.2), kind=kOutput, calls=%fused_computation.33 | convolution fusion | flops 537133056 | bytes 5505024 | tf_op jit(solution)/shard_map/dot_general | solution.py:41
  29.5 0.0 reduce-scatter.3.cloned.1.call-update
  29.6 0.7 fusion.63
  80.7 4.1 %multiply_reduce_fusion = (f32[128]{0:T(128)S(1)}, f32[128]{0:T(128)S(1)}, f32[128]{0:T(128)S(1)}, f32[128]{0:T(128)S(1)}, f32[128]{0:T(128)S(1)}, /*index=5*/f32[128]{0:T(128)S(1)}, f32[1024,128]{1,0:T(8,128)S(1)}) fusion(s32[]{:T(128)S(6)} %select_n.139, f32[1024,128]{1,0:T(8,128)S(1)} %convert_element_type.18, f32[128,128]{1,0:T(8,128)S(1)} %convert_element_type.19, ...), kind=kLoop, calls=%fused_computation.116 | loop fusion | flops 8912128 | bytes 1388608 | tf_op jit(solution)/shard_map/reduce_sum | solution.py:64
  84.8 0.5 multiply_reduce_fusion.12
  85.3 0.7 multiply_reduce_fusion.6
  86.0 1.3 %collective-permute-start.1 = (bf16[128,128]{1,0:T(8,128)(2,1)S(1)}, bf16[128,128]{1,0:T(8,128)(2,1)S(1)}, u32[]{:S(2)}, u32[]{:S(2)}) collective-permute-start(bf16[128,128]{1,0:T(8,128)(2,1)S(1)} %slice.203), channel_id=1, source_target_pairs={{2,0},{4,2},{6,4},{8,6},{10,8},{12,10},{14,12},{16,14},{18,16},{20... | collective-permute-start | bytes 98312 | tf_op jit(solution)/shard_map/ppermute | solution.py:16
  87.4 0.1 stack.2
  87.5 25.5 %all-gather = f32[256,128]{1,0:T(8,128)S(1)} all-gather(f32[16,128]{1,0:T(8,128)S(1)} %stack.2), channel_id=2, replica_groups=mesh['tm'=16,'series'=2] {'tm'}, dimensions={0}, use_global_device_ids=true | all-gather | bytes 139264 | tf_op jit(solution)/shard_map/all_gather | solution.py:67
  113.0 0.6 reduce_sum.169
  113.6 0.5 fusion.31
  114.2 3.3 %fusion.11 = f32[1024,128]{1,0:T(8,128)S(1)} fusion(f32[1024,128]{1,0:T(8,128)S(1)} %get-tuple-element.19, s32[]{:T(128)S(6)} %select_n.141, s32[]{:T(128)S(6)} %select_n.142, s32[]{:T(128)S(6)} %select_n.143, s32[]{:T(128)S(6)} %select_n.144, s32[]{:T(128)S(6)} %select_n.145, s32[]{:T(128)S(6)} %select_n.146, s32[]{:T(128)S(6)} %select_n.147, ...), kind=kLoop, calls=%fused_computation.78 | loop fusion | flops 3932160 | bytes 1119272 | tf_op jit(solution)/shard_map/sub | solution.py:62
  117.4 0.0 reduce-scatter.5.cloned.1.call-done
  117.4 2.2 %fusion.52 = f32[512,128]{1,0:T(8,128)} fusion(f32[512,128]{1,0:T(8,128)} %reduce-scatter.5.cloned.1.call-done, s32[]{:T(128)S(6)} %add.190, f32[1024,128]{1,0:T(8,128)S(1)} %get-tuple-element.19, s32[]{:T(128)S(6)} %add.184, s32[]{:T(128)S(6)} %add.186, s32[]{:T(128)S(6)} %add.188, f32[128,128]{1,0:T(8,128)S(1)} %convert_element_type.20, ...), kind=kLoop, calls=%fused_computation.136 | loop fusion | flops 1048576 | bytes 1903124 | tf_op jit(solution)/shard_map/add | solution.py:74
  (28 shorter events, 0.2 us)
Async XLA Ops:
  7.2 7.3 %copy-start = (bf16[2048,128]{1,0:T(8,128)(2,1)S(1)}, bf16[2048,128]{1,0:T(8,128)(2,1)}, u32[]{:S(2)}) copy-start(bf16[2048,128]{1,0:T(8,128)(2,1)} %param.7) | copy-start | bytes 1572868
  7.2 110.3 %reduce-scatter.5.cloned.1.call-start = ((), (), s32[]{:S(2)}) async-start(), calls=%async_computation.3 | async-start | bytes 786432 | tf_op jit(solution)/shard_map/reduce_scatter | solution.py:69
  18.6 1.9 %copy-start.1 = (bf16[2048,1024]{1,0:T(8,128)(2,1)}, bf16[2048,1024]{1,0:T(8,128)(2,1)S(1)}, u32[]{:S(2)}) copy-start(bf16[2048,1024]{1,0:T(8,128)(2,1)S(1)} %select_convert_fusion) | copy-start | bytes 12582916
  20.5 2.2 %copy-start.2 = (bf16[1024,128]{1,0:T(8,128)(2,1)S(1)}, bf16[1024,128]{1,0:T(8,128)(2,1)}, u32[]{:S(2)}) copy-start(bf16[1024,128]{1,0:T(8,128)(2,1)} %param.8) | copy-start | bytes 786436
  22.6 7.0 %copy-start.3 = (s32[16]{0:T(128)S(1)}, s32[16]{0:T(128)}, u32[]{:S(2)}) copy-start(s32[16]{0:T(128)} %param.11) | copy-start | bytes 196
  22.6 7.7 %copy-start.4 = (f32[16,128]{1,0:T(8,128)S(1)}, f32[16,128]{1,0:T(8,128)}, u32[]{:S(2)}) copy-start(f32[16,128]{1,0:T(8,128)} %param.9) | copy-start | bytes 24580
  22.6 97.0 %reduce-scatter.3.cloned.1.call-start = ((), (), s32[]{:S(2)}) async-start(), calls=%async_computation.2 | async-start | bytes 1114112 | tf_op jit(solution)/shard_map/reduce_scatter | solution.py:66
  22.7 58.0 %collective-permute-start = (bf16[128,128]{1,0:T(8,128)(2,1)S(1)}, bf16[128,128]{1,0:T(8,128)(2,1)S(1)}, u32[]{:S(2)}, u32[]{:S(2)}) collective-permute-start(bf16[128,128]{1,0:T(8,128)(2,1)S(1)} %slice.70), channel_id=1, source_target_pairs={{0,2},{2,4},{4,6},{6,8},{8,10},{10,12},{12,14},{14,16},{16,18},{18... | collective-permute-start | bytes 98312 | tf_op jit(solution)/shard_map/ppermute | solution.py:16
  86.0 27.6 %collective-permute-start.1 = (bf16[128,128]{1,0:T(8,128)(2,1)S(1)}, bf16[128,128]{1,0:T(8,128)(2,1)S(1)}, u32[]{:S(2)}, u32[]{:S(2)}) collective-permute-start(bf16[128,128]{1,0:T(8,128)(2,1)S(1)} %slice.203), channel_id=1, source_target_pairs={{2,0},{4,2},{6,4},{8,6},{10,8},{12,10},{14,12},{16,14},{18,16},{20... | collective-permute-start | bytes 98312 | tf_op jit(solution)/shard_map/ppermute | solution.py:16
Sparse Core Ops, SparseCore 0:
  22.8 17.3 reduce-scatter.4
  44.3 57.6 reduce-scatter.2
